TPU v7x, 256 devices: a whole 4x4x8 slice. The times are simulated.
256 devices in a mesh: wide: 32 (over y, x, core), narrow: 8 (over z).
Axes of the slice: x: 4, y: 4, z: 8, core: 2. Of those that a mesh axis runs over, the one named last changes fastest.
Arguments:
- constraint_rows: bfloat16 [512, 256, 1024], P(None, ('wide', 'narrow')), may hold values from -1 to 1
- metric: bfloat16 [1024, 1024], replicated, may hold values from -8 to 8, as said below
Outputs:
- factored: float32 [512, 256, 8, 128], P(None, 'wide', 'narrow')
Inputs may be any that keep to these rules, and one draw needn't show every extreme that they name: `metric`: symmetric and positive definite.
All inputs are finite; a program needn't handle non-finite values.
Results may differ from a plain program's by a relative error of at most 0.0052.
Values may be sent and summed in bfloat16 or wider, within the bound.
No kernel may reach another device: no remote copies, remote signals or barrier semaphores. Data moves between devices by JAX's collectives and lax.ppermute only.
A program may use at most 64 MiB of HBM per device.

v0:
```python
import jax
import jax.numpy as jnp
from jax import lax
from jax.sharding import PartitionSpec as P

P_SIZE = 1024
PB = 256
NPANEL = 2


def left_solve(factor_low, right_side):
    return jax.scipy.linalg.solve_triangular(factor_low, right_side, lower=True)


def strip_major(schur_slab, strips):
    row_count = schur_slab.shape[0]
    strip_len = schur_slab.shape[1] // strips
    reordered = schur_slab.reshape(row_count, strip_len, strips).transpose(0, 2, 1)
    return reordered.reshape(row_count, 1, strips, strip_len)


def local(constraint_rows, metric):
    groups = lax.axis_size(("wide", "narrow"))
    strips = lax.axis_size("narrow")
    row_count = constraint_rows.shape[0]
    panel_depth = P_SIZE // groups
    block_rows = PB // groups
    flat_rows = constraint_rows[:, 0, :]
    projected = jnp.dot(flat_rows, metric, preferred_element_type=jnp.float32).astype(jnp.bfloat16)
    gram_cols = jnp.einsum(
        "rn,kmn->rkm",
        projected,
        lax.all_gather(constraint_rows[:panel_depth], ("wide", "narrow"), axis=1, tiled=True),
        preferred_element_type=jnp.float32,
    )
    schur_slab = (gram_cols * gram_cols).reshape(row_count, P_SIZE)
    grid_block = lax.all_to_all(
        strip_major(schur_slab, strips), "narrow", split_axis=2, concat_axis=1, tiled=True
    )
    strip_len = P_SIZE // strips
    grid_rows = row_count * strips
    narrow_panel = PB // strips
    own_strip = lax.axis_index("narrow")
    flat_block = grid_block.reshape(grid_rows, strip_len)
    for panel_number in range(NPANEL):
        col_begin = panel_number * PB
        row_begin = col_begin // groups
        strip_begin = col_begin // strips
        strip_end = strip_begin + narrow_panel
        own_rows = flat_block.reshape(row_count, strips, strip_len)[
            row_begin : row_begin + block_rows, :, strip_begin:
        ]
        shared = lax.all_gather(own_rows, "wide", axis=1, tiled=True)
        shared = shared.reshape(PB, strip_len - strip_begin)
        diag_strip, row_strip = (
            lax.all_gather(shared[:, :narrow_panel], "narrow", axis=1, tiled=True),
            lax.all_gather(flat_block[:, strip_begin:strip_end], "narrow", axis=1, tiled=True),
        )
        diag_block = diag_strip.reshape(PB, strips, narrow_panel).transpose(0, 2, 1).reshape(PB, PB)
        panel_cols = (
            row_strip.reshape(grid_rows, strips, narrow_panel)
            .transpose(0, 2, 1)
            .reshape(grid_rows, PB)
        )
        factor_low = jnp.linalg.cholesky(diag_block)
        upper_part = left_solve(factor_low, shared[:, narrow_panel:])
        column = left_solve(factor_low, panel_cols.T).T
        trailing = flat_block[:, strip_end:] - jnp.dot(
            column, upper_part, precision=lax.Precision.HIGHEST
        )
        own_cols = lax.dynamic_index_in_dim(
            column.reshape(grid_rows, narrow_panel, strips), own_strip, 2, keepdims=False
        )
        flat_block = jnp.concatenate([flat_block[:, :strip_begin], own_cols, trailing], axis=1)
    return flat_block.reshape(row_count, strips, 1, strip_len)


def solution(mesh):
    placed = (P(None, ("wide", "narrow"), None), P())
    return jax.shard_map(
        local,
        mesh=mesh,
        in_specs=placed,
        out_specs=P(None, "wide", "narrow", None),
        check_vma=False,
    )
```

profile of v0, /device:TPU:4, one launch (start us, length us, event | category | flops | bytes accessed | tf_op | source)
XLA Modules:
  0.0 463.7 jit_solution(18273028846116087548)
XLA Ops:
  8.1 110.0 %all-gather.6.cloned.1.call-done = bf16[4,256,1024]{2,0,1:T(4,128)(2,1)} async-done(((bf16[4,1,1024]{2,0,1:T(4,128)(2,1)}), bf16[4,256,1024]{2,0,1:T(4,128)(2,1)}) %all-gather.6.cloned.1.call-update) | async-done | bytes 2097168 | tf_op jit(solution)/shard_map/all_gather | solution.py:33
  118.1 5.7 %fusion.8 = f32[512,4,256]{0,2,1:T(8,128)} fusion(bf16[4,256,1024]{2,0,1:T(4,128)(2,1)} %all-gather.6.cloned.1.call-done, bf16[1024,1024]{1,0:T(8,128)(2,1)S(1)} %copy-done, bf16[512,1,1024]{2,0,1:T(8,128)(2,1)} %param.5), kind=kOutput, calls=%fused_computation.22 | convolution fusion | flops 2148532224 | bytes 7340032 | tf_op jit(solution)/shard_map/rn,kmn->rkm/dot_general | solution.py:30
  125.8 56.3 %all_to_all.4 = f32[512,1,8,128]{3,1,0,2:T(1,128)S(1)} all-to-all(f32[512,1,8,128]{3,1,0,2:T(1,128)S(1)} %bitcast.153), channel_id=1, replica_groups=mesh['wide'=32,'narrow'=8] {'narrow'}, dimensions={2} | all-to-all | bytes 4194304 | tf_op jit(solution)/shard_map/all_to_all | solution.py:37
  186.8 23.0 %all-gather = f32[1,1,256,128]{3,2,1,0:T(8,128)S(1)} all-gather(f32[1,1,8,128]{3,2,1,0:T(8,128)S(1)} %bitcast.150), channel_id=2, replica_groups=mesh['wide'=32,'narrow'=8] {'wide'}, dimensions={2}, use_global_device_ids=true | all-gather | bytes 135168 | tf_op jit(solution)/shard_map/all_gather | solution.py:53
  210.1 26.7 %all_gather.23 = f32[256,256]{0,1:T(8,128)S(1)} all-gather(f32[256,32]{0,1:T(8,128)S(1)} %copy.64), channel_id=1, replica_groups=mesh['wide'=32,'narrow'=8] {'narrow'}, dimensions={1}, use_global_device_ids=true | all-gather | bytes 294912 | tf_op jit(solution)/shard_map/all_gather | solution.py:56
  237.3 11.7 %cholesky.130 = f32[128,128]{1,0:T(8,128)S(1)} custom-call(f32[128,128]{1,0:T(8,128)S(1)} %cholesky.194), custom_call_target="Cholesky" | custom-call | tf_op jit(solution)/shard_map/jit(cholesky)/cholesky | solution.py:65
  249.1 9.8 %custom-call.23 = f32[1,128,128]{1,2,0:T(8,128)S(1)} custom-call(f32[1,128,128]{2,1,0:T(8,128)S(1)} %get-tuple-element.66), custom_call_target="InvertDiagBlocksLowerTriangular" | custom-call | tf_op jit(solution)/shard_map/jit(cholesky)/cholesky | solution.py:65
  259.4 11.7 %cholesky.147 = f32[128,128]{1,0:T(8,128)S(1)} custom-call(f32[128,128]{1,0:T(8,128)S(1)} %convolution_subtract_fusion.5), custom_call_target="Cholesky" | custom-call | tf_op jit(solution)/shard_map/jit(cholesky)/cholesky | solution.py:65
  273.2 3.9 while.6
  277.1 19.7 %custom-call.24 = f32[2,128,128]{1,2,0:T(8,128)S(1)} custom-call(f32[2,128,128]{2,1,0:T(8,128)S(1)} %get-tuple-element.37), custom_call_target="InvertDiagBlocksLowerTriangular" | custom-call | tf_op jit(solution)/shard_map/jit(_solve_triangular)/triangular_solve | solution.py:12
  296.8 2.1 copy.83
  299.8 4.6 copy.99
  310.3 2.7 convolution_subtract_fusion.2
  316.0 24.0 %all-gather.1 = f32[256,96]{1,0:T(8,128)S(1)} all-gather(f32[8,96]{1,0:T(8,128)S(1)} %copy.73), channel_id=3, replica_groups=mesh['wide'=32,'narrow'=8] {'wide'}, dimensions={0}, use_global_device_ids=true | all-gather | bytes 101376 | tf_op jit(solution)/shard_map/all_gather | solution.py:53
  340.2 26.5 %all_gather.26 = f32[256,256]{0,1:T(8,128)S(1)} all-gather(f32[256,32]{0,1:T(8,128)S(1)} %copy.85), channel_id=1, replica_groups=mesh['wide'=32,'narrow'=8] {'narrow'}, dimensions={1}, use_global_device_ids=true | all-gather | bytes 294912 | tf_op jit(solution)/shard_map/all_gather | solution.py:56
  367.2 11.7 %cholesky.164 = f32[128,128]{1,0:T(8,128)S(1)} custom-call(f32[128,128]{1,0:T(8,128)S(1)} %cholesky.197), custom_call_target="Cholesky" | custom-call | tf_op jit(solution)/shard_map/jit(cholesky)/cholesky | solution.py:65
  378.9 9.8 %custom-call.25 = f32[1,128,128]{1,2,0:T(8,128)S(1)} custom-call(f32[1,128,128]{2,1,0:T(8,128)S(1)} %get-tuple-element.62), custom_call_target="InvertDiagBlocksLowerTriangular" | custom-call | tf_op jit(solution)/shard_map/jit(cholesky)/cholesky | solution.py:65
  389.3 11.7 %cholesky.181 = f32[128,128]{1,0:T(8,128)S(1)} custom-call(f32[128,128]{1,0:T(8,128)S(1)} %convolution_subtract_fusion.4), custom_call_target="Cholesky" | custom-call | tf_op jit(solution)/shard_map/jit(cholesky)/cholesky | solution.py:65
  403.6 3.9 while.7
  407.5 19.7 %custom-call.26 = f32[2,128,128]{1,2,0:T(8,128)S(1)} custom-call(f32[2,128,128]{2,1,0:T(8,128)S(1)} %get-tuple-element.38), custom_call_target="InvertDiagBlocksLowerTriangular" | custom-call | tf_op jit(solution)/shard_map/jit(_solve_triangular)/triangular_solve | solution.py:12
  427.2 2.0 fusion.1
  432.5 4.6 copy.98
  444.4 2.9 convolution_subtract_fusion.3
  451.5 5.5 %pad_maximum_fusion.4 = f32[512,8,1,128]{3,1,0,2:T(8,128)} fusion(f32[512,8,1,64]{3,1,0,2:T(8,128)} %bitcast.154, f32[512,8,1,32]{3,1,0,2:T(8,128)} %bitcast.152, f32[512,8,1,32]{3,1,0,2:T(8,128)} %bitcast.151), kind=kLoop, calls=%fused_computation.18 | loop fusion | flops 1048576 | bytes 4194304 | tf_op jit(solution)/shard_map/concatenate | solution.py:74
  (97 shorter events, 44.8 us)
Async XLA Ops:
  6.5 111.6 %copy-start = (bf16[1024,1024]{1,0:T(8,128)(2,1)S(1)}, bf16[1024,1024]{1,0:T(8,128)(2,1)}, u32[]{:S(2)}) copy-start(bf16[1024,1024]{1,0:T(8,128)(2,1)} %param.6) | copy-start | bytes 6291460
  6.5 111.6 %all-gather.6.cloned.1.call-start = ((), (), s32[]{:S(2)}) async-start(), calls=%async_computation.1 | async-start | bytes 2105344 | tf_op jit(solution)/shard_map/all_gather | solution.py:33
  8.0 291.7 %all-gather.8.cloned.1.call-start = ((), (), s32[]{:S(2)}) async-start(), calls=%async_computation.2 | async-start | bytes 4718592 | tf_op jit(solution)/shard_map/all_gather | solution.py:57
  182.1 1.3 copy-start.3
  184.8 247.6 %all-gather.10.cloned.1.call-start = ((), (), s32[]{:S(2)}) async-start(), calls=%async_computation.3 | async-start | bytes 4718592 | tf_op jit(solution)/shard_map/all_gather | solution.py:57
  184.9 1.9 slice-start
  237.0 59.8 %copy-start.4 = (f32[4096,96]{1,0:T(8,128)S(1)}, f32[4096,96]{1,0:T(8,128)}, u32[]{:S(2)}) copy-start(f32[4096,96]{1,0:T(8,128)} %slice.153) | copy-start | bytes 4718596
  308.3 2.0 copy-start.7
  310.3 2.8 copy-start.2
  313.0 1.1 copy-start.5
  442.9 1.4 copy-start.6
  451.5 5.5 %copy-start.1 = (bf16[1024,1024]{1,0:T(8,128)(2,1)S(1)}, bf16[1024,1024]{1,0:T(8,128)(2,1)}, u32[]{:S(2)}) copy-start(bf16[1024,1024]{1,0:T(8,128)(2,1)} %param.6) | copy-start | bytes 6291460
Sparse Core Ops, SparseCore 0:
  11.1 107.0 all-gather.5
  184.9 53.2 all-gather.7
  315.2 53.6 all-gather.9
where the time goes:
time: 469 us; the launch traced here: 464 us
  blocking collectives  157 us (33%)
  other arithmetic  116 us (25%)
  waiting for transfers between devices  110 us (23%)
  local copies, waits for them, and re-layouts  38.8 us (8%)
  matrix products  25.5 us (5%)
  between operations  16.2 us (3%)
    all_gather x1, waiting for transfers between devices, local(): lax.all_gather(constraint_rows[:panel_depth], ('wide', 'narrow'), axis=1,...  110 us
    another operation x13, other arithmetic, local(): factor_low = jnp.linalg.cholesky(diag_block)  68.6 us
    all_to_all x1, blocking collectives, local(): lax.all_to_all(strip_major(schur_slab, strips), 'narrow', split_axis=2, c...  56.3 us
    all_gather x2, blocking collectives, local(): lax.all_gather(shared[:, :narrow_panel], 'narrow', axis=1, tiled=True)  53.2 us
    all_gather x2, blocking collectives, local(): shared = lax.all_gather(own_rows, 'wide', axis=1, tiled=True)  47 us
    another operation x5, other arithmetic, left_solve(): return jax.scipy.linalg.solve_triangular(factor_low, right_side, lower=True)  39.4 us
    another operation x12, matrix products, left_solve(): return jax.scipy.linalg.solve_triangular(factor_low, right_side, lower=True)  13.2 us
  transfers between devices with their start and end apart: 3, of which 1 were waited for; matrix products, arithmetic and copies ran while one was open for 28% of the time, Pallas kernels for 0%

commit v1 on v0

--- a/solution.py
+++ b/solution.py
@@ -6,6 +6,11 @@
 P_SIZE = 1024
 PB = 256
 NPANEL = 2
+
+
+def all_by_exchange(shard, axis, dim):
+    repeated = jnp.stack([shard] * lax.axis_size(axis))
+    return jnp.concatenate(lax.all_to_all(repeated, axis, 0, 0), axis=dim)
 
 
 def left_solve(factor_low, right_side):
@@ -30,7 +35,7 @@
     gram_cols = jnp.einsum(
         "rn,kmn->rkm",
         projected,
-        lax.all_gather(constraint_rows[:panel_depth], ("wide", "narrow"), axis=1, tiled=True),
+        all_by_exchange(constraint_rows[:panel_depth], ("wide", "narrow"), 1),
         preferred_element_type=jnp.float32,
     )
     schur_slab = (gram_cols * gram_cols).reshape(row_count, P_SIZE)

time: 469 us -> 425 us (0.906)
  waiting for transfers between devices: 110 us -> 0.07 us
  blocking collectives: 157 us -> 221 us
    all_gather x1 -> x0, waiting for transfers between devices: 110 us -> none  [local(): lax.all_gather(constraint_rows[:panel_depth], ('wide', 'narrow'), axis=1,...]
    all_to_all x0 -> x1, blocking collectives: none -> 66.8 us  [all_by_exchange(): return jnp.concatenate(lax.all_to_all(repeated, axis, 0, 0), axis=dim)]
  transfers between devices with their start and end apart: 3 -> 2, of which waited for: 1 -> 0; matrix products, arithmetic and copies ran while one was open for 28% -> 31% of each run, Pallas kernels for 0% -> 0%
where the time goes in v1:
time: 425 us; the launch traced here: 419 us
  blocking collectives  221 us (52%)
  other arithmetic  116 us (27%)
  local copies, waits for them, and re-layouts  39.3 us (9%)
  matrix products  25.2 us (6%)
  between operations  16.8 us (4%)
    another operation x13, other arithmetic, local(): factor_low = jnp.linalg.cholesky(diag_block)  68.7 us
    all_to_all x1, blocking collectives, all_by_exchange(): return jnp.concatenate(lax.all_to_all(repeated, axis, 0, 0), axis=dim)  66.8 us
    all_to_all x1, blocking collectives, local(): lax.all_to_all(strip_major(schur_slab, strips), 'narrow', split_axis=2, c...  55.1 us
    all_gather x2, blocking collectives, local(): lax.all_gather(shared[:, :narrow_panel], 'narrow', axis=1, tiled=True)  53 us
    all_gather x2, blocking collectives, local(): shared = lax.all_gather(own_rows, 'wide', axis=1, tiled=True)  45.8 us
    another operation x5, other arithmetic, left_solve(): return jax.scipy.linalg.solve_triangular(factor_low, right_side, lower=True)  39.4 us
    another operation x12, matrix products, left_solve(): return jax.scipy.linalg.solve_triangular(factor_low, right_side, lower=True)  13.2 us
  transfers between devices with their start and end apart: 2, of which 0 were waited for; matrix products, arithmetic and copies ran while one was open for 31% of the time, Pallas kernels for 0%

profile of v1, /device:TPU:4, one launch (start us, length us, event | category | flops | bytes accessed | tf_op | source)
XLA Modules:
  0.0 418.6 jit_solution(18414694765294300255)
XLA Ops:
  8.0 66.8 %all_to_all.14 = bf16[256,4,1,1024]{3,1,2,0:T(4,128)(2,1)} all-to-all(bf16[256,4,1,1024]{3,1,2,0:T(4,128)(2,1)S(1)} %stack.2), channel_id=1, replica_groups=mesh['wide'=32,'narrow'=8] {'wide','narrow'}, dimensions={0} | all-to-all | bytes 4194304 | tf_op jit(solution)/shard_map/all_to_all | solution.py:13
  74.8 5.4 %fusion.9 = f32[512,4,256]{0,2,1:T(8,128)} fusion(bf16[256,4,1,1024]{3,1,2,0:T(4,128)(2,1)} %all_to_all.14, bf16[1024,1024]{1,0:T(8,128)(2,1)S(1)} %copy-done, bf16[512,1,1024]{2,0,1:T(8,128)(2,1)S(1)} %copy-done.8), kind=kOutput, calls=%fused_computation.23 | convolution fusion | flops 2148532224 | bytes 7340032 | tf_op jit(solution)/shard_map/rn,kmn->rkm/dot_general | solution.py:35
  82.1 55.1 %all_to_all.15 = f32[512,1,8,128]{3,1,0,2:T(1,128)S(1)} all-to-all(f32[512,1,8,128]{3,1,0,2:T(1,128)S(1)} %bitcast.162), channel_id=1, replica_groups=mesh['wide'=32,'narrow'=8] {'narrow'}, dimensions={2} | all-to-all | bytes 4194304 | tf_op jit(solution)/shard_map/all_to_all | solution.py:42
  141.9 21.9 %all-gather = f32[1,1,256,128]{3,2,1,0:T(8,128)S(1)} all-gather(f32[1,1,8,128]{3,2,1,0:T(8,128)S(1)} %bitcast.159), channel_id=2, replica_groups=mesh['wide'=32,'narrow'=8] {'wide'}, dimensions={2}, use_global_device_ids=true | all-gather | bytes 135168 | tf_op jit(solution)/shard_map/all_gather | solution.py:58
  164.1 26.5 %all_gather.19 = f32[256,256]{0,1:T(8,128)S(1)} all-gather(f32[256,32]{0,1:T(8,128)S(1)} %copy.61), channel_id=1, replica_groups=mesh['wide'=32,'narrow'=8] {'narrow'}, dimensions={1}, use_global_device_ids=true | all-gather | bytes 294912 | tf_op jit(solution)/shard_map/all_gather | solution.py:61
  191.1 11.7 %cholesky.130 = f32[128,128]{1,0:T(8,128)S(1)} custom-call(f32[128,128]{1,0:T(8,128)S(1)} %cholesky.194), custom_call_target="Cholesky" | custom-call | tf_op jit(solution)/shard_map/jit(cholesky)/cholesky | solution.py:70
  202.9 9.8 %custom-call.23 = f32[1,128,128]{1,2,0:T(8,128)S(1)} custom-call(f32[1,128,128]{2,1,0:T(8,128)S(1)} %get-tuple-element.66), custom_call_target="InvertDiagBlocksLowerTriangular" | custom-call | tf_op jit(solution)/shard_map/jit(cholesky)/cholesky | solution.py:70
  213.2 11.7 %cholesky.147 = f32[128,128]{1,0:T(8,128)S(1)} custom-call(f32[128,128]{1,0:T(8,128)S(1)} %convolution_subtract_fusion.5), custom_call_target="Cholesky" | custom-call | tf_op jit(solution)/shard_map/jit(cholesky)/cholesky | solution.py:70
  227.1 4.2 while.6
  231.3 19.7 %custom-call.24 = f32[2,128,128]{1,2,0:T(8,128)S(1)} custom-call(f32[2,128,128]{2,1,0:T(8,128)S(1)} %get-tuple-element.37), custom_call_target="InvertDiagBlocksLowerTriangular" | custom-call | tf_op jit(solution)/shard_map/jit(_solve_triangular)/triangular_solve | solution.py:17
  251.0 2.1 copy.80
  254.0 4.6 %copy.98 = f32[4096,32,8]{0,2,1:T(8,128)S(1)} copy(f32[4096,32,8]{0,1,2:T(8,128)} %bitcast.165) | data formatting | bytes 8388608 | tf_op jit(solution)/shard_map/transpose | solution.py:67
  264.5 2.7 convolution_subtract_fusion.2
  270.2 23.9 %all-gather.1 = f32[256,96]{1,0:T(8,128)S(1)} all-gather(f32[8,96]{1,0:T(8,128)S(1)} %copy.70), channel_id=3, replica_groups=mesh['wide'=32,'narrow'=8] {'wide'}, dimensions={0}, use_global_device_ids=true | all-gather | bytes 101376 | tf_op jit(solution)/shard_map/all_gather | solution.py:58
  294.3 26.5 %all_gather.22 = f32[256,256]{0,1:T(8,128)S(1)} all-gather(f32[256,32]{0,1:T(8,128)S(1)} %copy.82), channel_id=1, replica_groups=mesh['wide'=32,'narrow'=8] {'narrow'}, dimensions={1}, use_global_device_ids=true | all-gather | bytes 294912 | tf_op jit(solution)/shard_map/all_gather | solution.py:61
  321.3 11.7 %cholesky.164 = f32[128,128]{1,0:T(8,128)S(1)} custom-call(f32[128,128]{1,0:T(8,128)S(1)} %cholesky.197), custom_call_target="Cholesky" | custom-call | tf_op jit(solution)/shard_map/jit(cholesky)/cholesky | solution.py:70
  333.1 9.8 %custom-call.25 = f32[1,128,128]{1,2,0:T(8,128)S(1)} custom-call(f32[1,128,128]{2,1,0:T(8,128)S(1)} %get-tuple-element.62), custom_call_target="InvertDiagBlocksLowerTriangular" | custom-call | tf_op jit(solution)/shard_map/jit(cholesky)/cholesky | solution.py:70
  343.4 11.7 %cholesky.181 = f32[128,128]{1,0:T(8,128)S(1)} custom-call(f32[128,128]{1,0:T(8,128)S(1)} %convolution_subtract_fusion.4), custom_call_target="Cholesky" | custom-call | tf_op jit(solution)/shard_map/jit(cholesky)/cholesky | solution.py:70
  357.9 4.1 while.7
  362.0 19.7 %custom-call.26 = f32[2,128,128]{1,2,0:T(8,128)S(1)} custom-call(f32[2,128,128]{2,1,0:T(8,128)S(1)} %get-tuple-element.38), custom_call_target="InvertDiagBlocksLowerTriangular" | custom-call | tf_op jit(solution)/shard_map/jit(_solve_triangular)/triangular_solve | solution.py:17
  381.7 2.0 fusion.1
  387.0 4.6 %copy.97 = f32[4096,8,32]{0,1,2:T(8,128)S(1)} copy(f32[4096,8,32]{0,2,1:T(8,128)} %bitcast.164) | data formatting | bytes 8388608 | tf_op jit(solution)/shard_map/reshape | solution.py:66
  398.9 2.9 convolution_subtract_fusion.3
  405.9 5.5 %pad_maximum_fusion.4 = f32[512,8,1,128]{3,1,0,2:T(8,128)} fusion(f32[512,8,1,64]{3,1,0,2:T(8,128)} %bitcast.163, f32[512,8,1,32]{3,1,0,2:T(8,128)} %bitcast.161, f32[512,8,1,32]{3,1,0,2:T(8,128)} %bitcast.160), kind=kLoop, calls=%fused_computation.18 | loop fusion | flops 1048576 | bytes 4194304 | tf_op jit(solution)/shard_map/concatenate | solution.py:79
  (98 shorter events, 45.3 us)
Async XLA Ops:
  6.5 68.2 %copy-start = (bf16[1024,1024]{1,0:T(8,128)(2,1)S(1)}, bf16[1024,1024]{1,0:T(8,128)(2,1)}, u32[]{:S(2)}) copy-start(bf16[1024,1024]{1,0:T(8,128)(2,1)} %param.6) | copy-start | bytes 6291460
  6.5 247.4 %all-gather.5.cloned.1.call-start = ((), (), s32[]{:S(2)}) async-start(), calls=%async_computation.2 | async-start | bytes 4718592 | tf_op jit(solution)/shard_map/all_gather | solution.py:62
  8.0 66.8 %copy-start.8 = (bf16[512,1,1024]{2,0,1:T(8,128)(2,1)S(1)}, bf16[512,1,1024]{2,0,1:T(8,128)(2,1)}, u32[]{:S(2)}) copy-start(bf16[512,1,1024]{2,0,1:T(8,128)(2,1)} %param.5) | copy-start | bytes 3145732
  137.2 1.3 copy-start.3
  139.9 247.0 %all-gather.7.cloned.1.call-start = ((), (), s32[]{:S(2)}) async-start(), calls=%async_computation.3 | async-start | bytes 4718592 | tf_op jit(solution)/shard_map/all_gather | solution.py:62
  140.0 1.9 slice-start
  190.8 60.2 %copy-start.4 = (f32[4096,96]{1,0:T(8,128)S(1)}, f32[4096,96]{1,0:T(8,128)}, u32[]{:S(2)}) copy-start(f32[4096,96]{1,0:T(8,128)} %slice.156) | copy-start | bytes 4718596
  262.5 2.0 copy-start.7
  264.5 2.8 copy-start.2
  267.2 1.1 copy-start.5
  397.5 1.4 copy-start.6
  405.9 5.5 %copy-start.1 = (bf16[1024,1024]{1,0:T(8,128)(2,1)S(1)}, bf16[1024,1024]{1,0:T(8,128)(2,1)}, u32[]{:S(2)}) copy-start(bf16[1024,1024]{1,0:T(8,128)(2,1)} %param.6) | copy-start | bytes 6291460
Sparse Core Ops, SparseCore 0:
  140.1 51.4 all-gather.4
  269.4 53.5 all-gather.6
